TPU v7x, 32 devices: a whole 2x2x4 slice. The times are simulated.
32 devices in a mesh: tensor: 4 (over z), frames: 2 (over core), batch: 4 (over y, x).
Axes of the slice: x: 2, y: 2, z: 4, core: 2. Of those that a mesh axis runs over, the one named last changes fastest.
Arguments:
- tokens: bfloat16 [4, 2, 1024, 1024], P('batch', 'frames', 'tensor'), may hold values from -6 to 6
- cotangent: bfloat16 [4, 2, 1024, 1024], P('batch', 'frames', 'tensor'), may hold values from -6 to 6
- bucket: int32 [4], P('batch'), may hold values from 0 to 1, as said below
- clip_of_frame: int32 [4, 8], P('batch'), may hold values from 0 to 6, as said below
- noise_index: int32 [4, 8], P('batch'), may hold values from 0 to 999
- noise_table: float32 [1000, 1024], replicated, may hold values from -6 to 6
- w_mod: bfloat16 [1024, 6144], P(None, 'tensor'), may hold values from -0.1875 to 0.1875
- b_mod: bfloat16 [6144], P('tensor'), may hold values from -1.796875 to 1.796875
- w_qkv: bfloat16 [1024, 3, 1024], P(None, None, 'tensor'), may hold values from -0.1875 to 0.1875
- w_out: bfloat16 [1024, 1024], P('tensor'), may hold values from -1 to 1
- w_up: bfloat16 [1024, 4096], P(None, 'tensor'), may hold values from -0.1875 to 0.1875
- w_down: bfloat16 [4096, 1024], P('tensor'), may hold values from -0.09375 to 0.09375
Outputs:
- out: bfloat16 [4, 2, 1024, 1024], P('batch', 'frames', 'tensor')
- d_tokens: bfloat16 [4, 2, 1024, 1024], P('batch', 'frames', 'tensor')
- d_w_mod: float32 [1024, 6144], P(None, 'tensor')
- d_b_mod: float32 [6144], P('tensor')
- d_w_qkv: float32 [1024, 3, 1024], P(None, None, 'tensor')
- d_w_out: float32 [1024, 1024], P('tensor')
- d_w_up: float32 [1024, 4096], P(None, 'tensor')
- d_w_down: float32 [4096, 1024], P('tensor')
Inputs may be any that keep to these rules, and one draw needn't show every extreme that they name: `bucket`: both values occur in every draw. `clip_of_frame`: A row starts at 0 and never falls; with F the row's frame count (2048 divided by its frame size), frames F // 2 - 1 and F // 2 share a clip; entries from frame F on repeat the clip of frame F - 1. In some pack of 16 by 16 patches every other frame starts a clip of its own. `noise_index`: only a row's first 2048 / (frame size) entries are read.
All inputs are finite; a program needn't handle non-finite values.
Results may differ from a plain program's by a relative error of at most 0.017.
The roundings to bfloat16 on the way count: a program that leaves them out, or rounds other values in their place, can miss the bound.
Values may be sent and summed in bfloat16 or wider, within the bound.
No kernel may reach another device: no remote copies, remote signals or barrier semaphores. Data moves between devices by JAX's collectives and lax.ppermute only.
A program may use at most 192 MiB of HBM per device.

v0:
```python
import jax
import jax.numpy as jnp
from jax import lax
from jax.sharding import PartitionSpec as P

HEAD_DIM = 64
FRAME_SMALL = 256
FRAME_LARGE = 1024
eps = 1e-06
highest = lax.Precision.HIGHEST


def from_behind(value, axis, steps):
    count = lax.axis_size(axis)
    initial, last = (max(0, -steps), min(count, count - steps))
    return lax.ppermute(value, axis, [(source, source + steps) for source in range(initial, last)])


def normalize(values):
    centre = values - jnp.mean(values, axis=-1, keepdims=True)
    spread = jnp.mean(centre * centre, axis=-1, keepdims=True)
    inverse = lax.rsqrt(spread + eps)
    return (centre * inverse, inverse)


def norm_back(grad, normed, inverse):
    mean_grad = jnp.mean(grad, axis=-1, keepdims=True)
    mean_mix = jnp.mean(grad * normed, axis=-1, keepdims=True)
    return inverse * (grad - mean_grad - normed * mean_mix)


def rotary(positions):
    half_dim = HEAD_DIM // 2
    frequency = 10000.0 ** (-(jnp.arange(half_dim, dtype=jnp.float32) * 2.0 / HEAD_DIM))
    angles = positions.astype(jnp.float32)[:, None] * frequency[None, :]
    cosine = jnp.concatenate([jnp.cos(angles), jnp.cos(angles)], axis=-1)[:, None, :]
    sine_table = jnp.concatenate([jnp.sin(angles), jnp.sin(angles)], axis=-1)[:, None, :]
    return (cosine, sine_table)


def rotate(values, cosine, sine_table):
    half_dim = values.shape[-1] // 2
    turned = jnp.concatenate([-values[..., half_dim:], values[..., :half_dim]], axis=-1)
    return values * cosine + turned * sine_table


def gelu_back(pre, grad_hidden):
    return jax.vjp(lambda inner: jax.nn.gelu(inner, approximate=True), pre)[1](grad_hidden)[0]


def spread_rows(rows):
    return lax.all_gather(rows, "tensor", axis=0, tiled=True)


def collect_rows(left_rows, right_matrix, contract):
    return lax.psum_scatter(
        lax.dot_general(
            left_rows,
            right_matrix,
            (((1,), (contract,)), ((), ())),
            preferred_element_type=jnp.float32,
        ),
        "tensor",
        scatter_dimension=0,
        tiled=True,
    )


def masked_scores(query_block, frame_query, clip_query, all_keys, key_frame, key_clip, score_scale):
    allowed = (clip_query[:, None] == key_clip[None, :]) & (
        key_frame[None, :] <= frame_query[:, None]
    )
    scores = (
        jnp.einsum("qhd,khd->hqk", query_block, all_keys, preferred_element_type=jnp.float32)
        * score_scale
    )
    return jnp.where(allowed[None], scores, -1e30)


def attend(
    query_block, frame_query, clip_query, all_keys, all_values, key_frame, key_clip, score_scale
):
    scores = masked_scores(
        query_block, frame_query, clip_query, all_keys, key_frame, key_clip, score_scale
    )
    row_max = jnp.max(scores, axis=-1, keepdims=True)
    weights_exp = jnp.exp(scores - row_max)
    row_total = jnp.sum(weights_exp, axis=-1, keepdims=True)
    probabilities = (weights_exp / row_total).astype(jnp.bfloat16)
    mixed = jnp.einsum(
        "hqk,khd->qhd", probabilities, all_values, preferred_element_type=jnp.float32
    )
    return (mixed, (row_max + jnp.log(row_total))[..., 0])


def attend_back(
    query_block,
    frame_query,
    clip_query,
    grad_mixed,
    log_total,
    all_keys,
    all_values,
    key_frame,
    key_clip,
    score_scale,
):
    scores = masked_scores(
        query_block, frame_query, clip_query, all_keys, key_frame, key_clip, score_scale
    )
    probabilities = jnp.exp(scores - log_total[..., None])
    grad_probs = jnp.einsum(
        "qhd,khd->hqk", grad_mixed, all_values, preferred_element_type=jnp.float32
    )
    centre = jnp.sum(probabilities * grad_probs, axis=-1, keepdims=True)
    grad_scores = (probabilities * (grad_probs - centre)).astype(jnp.bfloat16)
    grad_query = (
        jnp.einsum("hqk,khd->qhd", grad_scores, all_keys, preferred_element_type=jnp.float32)
        * score_scale
    )
    grad_keys = (
        jnp.einsum("hqk,qhd->khd", grad_scores, query_block, preferred_element_type=jnp.float32)
        * score_scale
    )
    grad_values = jnp.einsum(
        "hqk,qhd->khd",
        probabilities.astype(jnp.bfloat16),
        grad_mixed,
        preferred_element_type=jnp.float32,
    )
    return (grad_query, grad_keys, grad_values)


def local(
    tokens,
    cotangent,
    bucket,
    clip_of_frame,
    noise_index,
    noise_table,
    w_mod,
    b_mod,
    w_qkv,
    w_out,
    w_up,
    w_down,
):
    tensor_size = lax.axis_size("tensor")
    tensor_rank = lax.axis_index("tensor")
    frame_rank = lax.axis_index("frames")
    local_rows = tokens.shape[2]
    model_width = tokens.shape[3]
    shard_rows = local_rows * tensor_size
    width_local = w_qkv.shape[2]
    heads_local = width_local // HEAD_DIM
    frame_slots = clip_of_frame.shape[1]
    clip_row = clip_of_frame[0]
    level_row = noise_index[0]
    frame_size = jnp.where(bucket[0] == 0, FRAME_SMALL, FRAME_LARGE).astype(jnp.int32)
    shard_start = frame_rank * shard_rows
    shard_pos = shard_start + jnp.arange(shard_rows, dtype=jnp.int32)
    local_pos = shard_start + tensor_rank * local_rows + jnp.arange(local_rows, dtype=jnp.int32)
    local_frame = local_pos // frame_size
    shard_frame = shard_pos // frame_size
    shard_clip = jnp.take(clip_row, shard_frame)
    past_pos = shard_pos - shard_rows
    past_frame = jnp.maximum(past_pos, 0) // frame_size
    past_clip = jnp.where(past_pos >= 0, jnp.take(clip_row, past_frame), -1)
    key_frame = jnp.concatenate([past_frame, shard_frame])
    key_clip = jnp.concatenate([past_clip, shard_clip])
    cond = jax.nn.silu(jnp.take(noise_table, level_row, axis=0)).astype(jnp.bfloat16)
    mod_part = (
        jnp.dot(cond, w_mod, preferred_element_type=jnp.float32)
        + b_mod.astype(jnp.float32)[None, :]
    )
    mod_whole = lax.all_gather(mod_part, "tensor", axis=1, tiled=True)
    selector = (local_frame[:, None] == jnp.arange(frame_slots, dtype=jnp.int32)[None, :]).astype(
        jnp.float32
    )
    per_token = jnp.dot(selector, mod_whole, precision=highest)
    shift_one = per_token[:, 0:model_width]
    scale_one = per_token[:, model_width : 2 * model_width]
    gate_one = per_token[:, 2 * model_width : 3 * model_width]
    shift_two = per_token[:, 3 * model_width : 4 * model_width]
    scale_two = per_token[:, 4 * model_width : 5 * model_width]
    gate_two = per_token[:, 5 * model_width : 6 * model_width]
    residual = tokens[0, 0].astype(jnp.float32)
    normed_one, inverse_one = normalize(residual)
    attn_in = (normed_one * (1.0 + scale_one) + shift_one).astype(jnp.bfloat16)
    attn_whole = spread_rows(attn_in)
    projected = jnp.einsum("sd,dcf->scf", attn_whole, w_qkv, preferred_element_type=jnp.float32)
    cosine, sine_table = rotary(shard_pos)
    q_raw = projected[:, 0].reshape(shard_rows, heads_local, HEAD_DIM)
    k_raw = projected[:, 1].reshape(shard_rows, heads_local, HEAD_DIM)
    queries = rotate(q_raw, cosine, sine_table).astype(jnp.bfloat16)
    own_keys = rotate(k_raw, cosine, sine_table).astype(jnp.bfloat16)
    own_values = projected[:, 2].reshape(shard_rows, heads_local, HEAD_DIM).astype(jnp.bfloat16)
    past_keys, past_values = from_behind((own_keys, own_values), "frames", 1)
    all_keys = jnp.concatenate([past_keys, own_keys], axis=0)
    all_values = jnp.concatenate([past_values, own_values], axis=0)
    score_scale = HEAD_DIM ** (-0.5)
    block_rows = min(512, shard_rows)
    block_count = shard_rows // block_rows
    query_blocks = queries.reshape(block_count, block_rows, heads_local, HEAD_DIM)
    frame_blocks = shard_frame.reshape(block_count, block_rows)
    clip_blocks = shard_clip.reshape(block_count, block_rows)

    def forward_block(block_items):
        return attend(
            block_items[0],
            block_items[1],
            block_items[2],
            all_keys,
            all_values,
            key_frame,
            key_clip,
            score_scale,
        )

    attn_blocks, total_blocks = lax.map(forward_block, (query_blocks, frame_blocks, clip_blocks))
    attn_rows = attn_blocks.reshape(shard_rows, width_local).astype(jnp.bfloat16)
    branch_one = collect_rows(attn_rows, w_out, 0)
    mixed_one = residual + gate_one * branch_one
    normed_two, inverse_two = normalize(mixed_one)
    mlp_in = (normed_two * (1.0 + scale_two) + shift_two).astype(jnp.bfloat16)
    mlp_whole = spread_rows(mlp_in)
    pre = jnp.dot(mlp_whole, w_up, preferred_element_type=jnp.float32)
    hidden = jax.nn.gelu(pre, approximate=True).astype(jnp.bfloat16)
    branch_two = collect_rows(hidden, w_down, 0)
    result = (mixed_one + gate_two * branch_two).astype(jnp.bfloat16)
    grad_out = cotangent[0, 0].astype(jnp.float32)
    grad_branch_two = (gate_two * grad_out).astype(jnp.bfloat16)
    grad_gate_two = grad_out * branch_two
    grad_two_whole = spread_rows(grad_branch_two)
    mlp_source, _ = lax.optimization_barrier((mlp_in, grad_branch_two))
    mlp_again = spread_rows(mlp_source)
    grad_hidden = lax.dot_general(
        grad_two_whole, w_down, (((1,), (1,)), ((), ())), preferred_element_type=jnp.float32
    )
    grad_pre = gelu_back(pre, grad_hidden).astype(jnp.bfloat16)
    grad_w_down = lax.dot_general(
        hidden, grad_two_whole, (((0,), (0,)), ((), ())), preferred_element_type=jnp.float32
    )
    grad_w_up = lax.dot_general(
        mlp_again, grad_pre, (((0,), (0,)), ((), ())), preferred_element_type=jnp.float32
    )
    grad_mlp_in = collect_rows(grad_pre, w_up, 1)
    grad_scale_two = grad_mlp_in * normed_two
    grad_mixed_one = grad_out + norm_back(grad_mlp_in * (1.0 + scale_two), normed_two, inverse_two)
    grad_branch_one = (gate_one * grad_mixed_one).astype(jnp.bfloat16)
    grad_gate_one = grad_mixed_one * branch_one
    grad_one_whole = spread_rows(grad_branch_one)
    grad_attn = lax.dot_general(
        grad_one_whole, w_out, (((1,), (1,)), ((), ())), preferred_element_type=jnp.float32
    ).astype(jnp.bfloat16)
    grad_w_out = lax.dot_general(
        attn_rows, grad_one_whole, (((0,), (0,)), ((), ())), preferred_element_type=jnp.float32
    )
    grad_attn_blocks = grad_attn.reshape(block_count, block_rows, heads_local, HEAD_DIM)

    def backward_block(carry, block_items):
        query_block, frame_query, clip_query, grad_mixed, log_total = block_items
        grad_query, grad_keys, grad_values = attend_back(
            query_block,
            frame_query,
            clip_query,
            grad_mixed,
            log_total,
            all_keys,
            all_values,
            key_frame,
            key_clip,
            score_scale,
        )
        return ((carry[0] + grad_keys, carry[1] + grad_values), grad_query)

    zero_keys = jnp.zeros((2 * shard_rows, heads_local, HEAD_DIM), jnp.float32)
    key_sums, query_grads = lax.scan(
        backward_block,
        (zero_keys, zero_keys),
        (query_blocks, frame_blocks, clip_blocks, grad_attn_blocks, total_blocks),
    )
    back_keys, back_values = (
        from_behind(key_sums[0][:shard_rows].astype(jnp.bfloat16), "frames", -1).astype(
            jnp.float32
        ),
        from_behind(key_sums[1][:shard_rows].astype(jnp.bfloat16), "frames", -1).astype(
            jnp.float32
        ),
    )
    own_key_grads = key_sums[0][shard_rows:] + back_keys
    own_value_grads = key_sums[1][shard_rows:] + back_values
    grad_q_raw = rotate(query_grads.reshape(shard_rows, heads_local, HEAD_DIM), cosine, -sine_table)
    grad_k_raw = rotate(own_key_grads, cosine, -sine_table)
    grad_qkv = jnp.stack(
        [
            grad_q_raw.reshape(shard_rows, width_local),
            grad_k_raw.reshape(shard_rows, width_local),
            own_value_grads.reshape(shard_rows, width_local),
        ],
        axis=1,
    ).astype(jnp.bfloat16)
    attn_source, _ = lax.optimization_barrier((attn_in, grad_attn))
    attn_again = spread_rows(attn_source)
    grad_w_qkv = jnp.einsum("sd,scf->dcf", attn_again, grad_qkv, preferred_element_type=jnp.float32)
    grad_attn_in = collect_rows(
        grad_qkv.reshape(shard_rows, 3 * width_local),
        w_qkv.reshape(model_width, 3 * width_local),
        1,
    )
    grad_scale_one = grad_attn_in * normed_one
    grad_tokens = grad_mixed_one + norm_back(
        grad_attn_in * (1.0 + scale_one), normed_one, inverse_one
    )
    grad_token_mod = jnp.concatenate(
        [grad_attn_in, grad_scale_one, grad_gate_one, grad_mlp_in, grad_scale_two, grad_gate_two],
        axis=1,
    )
    grad_frame_mod = lax.dot_general(
        selector, grad_token_mod, (((0,), (0,)), ((), ())), precision=highest
    )
    mod_share = lax.psum_scatter(
        grad_frame_mod.astype(jnp.bfloat16), "tensor", scatter_dimension=1, tiled=True
    ).astype(jnp.float32)
    grad_w_mod = lax.dot_general(
        cond.astype(jnp.float32), mod_share, (((0,), (0,)), ((), ())), precision=highest
    )
    grad_b_mod = jnp.sum(mod_share, axis=0)
    summed = (
        lax.psum(grad_w_mod.astype(jnp.bfloat16), ("frames", "batch")).astype(jnp.float32),
        lax.psum(grad_b_mod.astype(jnp.bfloat16), ("frames", "batch")).astype(jnp.float32),
        lax.psum(grad_w_qkv.astype(jnp.bfloat16), ("frames", "batch")).astype(jnp.float32),
        lax.psum(grad_w_out.astype(jnp.bfloat16), ("frames", "batch")).astype(jnp.float32),
        lax.psum(grad_w_up.astype(jnp.bfloat16), ("frames", "batch")).astype(jnp.float32),
        lax.psum(grad_w_down.astype(jnp.bfloat16), ("frames", "batch")).astype(jnp.float32),
    )
    return (
        result.reshape(1, 1, local_rows, model_width),
        grad_tokens.astype(jnp.bfloat16).reshape(1, 1, local_rows, model_width),
        summed[0],
        summed[1],
        summed[2],
        summed[3],
        summed[4],
        summed[5],
    )


def solution(mesh):
    placed = (
        P("batch", "frames", "tensor", None),
        P("batch", "frames", "tensor", None),
        P("batch"),
        P("batch", None),
        P("batch", None),
        P(),
        P(None, "tensor"),
        P("tensor"),
        P(None, None, "tensor"),
        P("tensor", None),
        P(None, "tensor"),
        P("tensor", None),
    )
    return jax.shard_map(
        local,
        mesh=mesh,
        in_specs=placed,
        out_specs=(
            P("batch", "frames", "tensor", None),
            P("batch", "frames", "tensor", None),
            P(None, "tensor"),
            P("tensor"),
            P(None, None, "tensor"),
            P("tensor", None),
            P(None, "tensor"),
            P("tensor", None),
        ),
        check_vma=False,
    )
```

profile of v0, /device:TPU:0, one launch (start us, length us, event | category | flops | bytes accessed | tf_op | source)
XLA Modules:
  0.0 981.8 jit_solution(5190104987393337398)
XLA Ops:
  16.0 15.6 %all_gather.21 = f32[8,6144]{1,0:T(8,128)S(1)} all-gather(f32[8,1536]{1,0:T(8,128)S(1)} %convolution_add_fusion), channel_id=1, replica_groups=mesh['tensor'=4,'frames'=2,'batch'=4] {'tensor'}, dimensions={1}, use_global_device_ids=true | all-gather | bytes 245760 | tf_op jit(solution)/shard_map/all_gather | solution.py:176
  51.4 34.1 %all-gather.7.cloned.1.call-done = bf16[1024,1024]{1,0:T(8,128)(2,1)} async-done(((bf16[256,1024]{1,0:T(8,128)(2,1)}), bf16[1024,1024]{1,0:T(8,128)(2,1)}) %all-gather.7.cloned.1.call-update) | async-done | bytes 2097168 | tf_op jit(solution)/shard_map/all_gather | solution.py:52
  104.5 29.2 %while.29 = (s32[]{:T(128)}, bf16[2,512,4,64]{1,3,2,0:T(8,128)(2,1)S(1)}, f32[2,4,512]{2,1,0:T(4,128)}, s32[2,512]{1,0:T(2,128)S(1)}, s32[2048]{0:T(1024)S(1)}, ...) while((s32[]{:T(128)}, ...), condition=%wide.region_5.7_spmd.clone, body=%wide.region_2.6_spmd.sunk.clone | while | flops 1127217152 | bytes 57503868 | solution.py:220
  139.0 75.9 %reduce-scatter.6.cloned.1.call-done = f32[256,1024]{1,0:T(8,128)} async-done(((f32[1024,1024]{1,0:T(8,128)}), f32[256,1024]{1,0:T(8,128)}) %reduce-scatter.6.cloned.1.call-update) | async-done | bytes 1048592 | tf_op jit(solution)/shard_map/reduce_scatter | solution.py:56
  221.9 45.3 %all-gather.11.cloned.1.call-done = bf16[1024,1024]{1,0:T(8,128)(2,1)} async-done(((bf16[256,1024]{1,0:T(8,128)(2,1)}), bf16[1024,1024]{1,0:T(8,128)(2,1)}) %all-gather.11.cloned.1.call-update) | async-done | bytes 2097168 | tf_op jit(solution)/shard_map/all_gather | solution.py:52
  273.8 39.3 %all-gather.9.cloned.1.call-done = bf16[1024,1024]{1,0:T(8,128)(2,1)} async-done(((bf16[256,1024]{1,0:T(8,128)(2,1)}), bf16[1024,1024]{1,0:T(8,128)(2,1)}) %all-gather.9.cloned.1.call-update) | async-done | bytes 2097168 | tf_op jit(solution)/shard_map/all_gather | solution.py:52
  313.1 10.0 %fusion.47 = (bf16[1024,1024]{1,0:T(8,128)(2,1)S(1)}, f32[1024,1024]{1,0:T(8,128)}) fusion(f32[1024,1024]{1,0:T(8,128)} %fusion.107, bf16[1024,1024]{1,0:T(8,128)(2,1)} %all-gather.9.cloned.1.call-done, bf16[1024,1024]{1,0:T(8,128)(2,1)} %param.28), kind=kOutput, calls=%fused_computation.62 | convolution fusion | flops 2168455168 | bytes 14680064 | tf_op jit(solution)/shard_map/dot_general | solution.py:227
  328.9 7.5 fusion.101
  336.5 68.1 %reduce-scatter.10.cloned.1.call-done = f32[256,1024]{1,0:T(8,128)} async-done(((f32[1024,1024]{1,0:T(8,128)}), f32[256,1024]{1,0:T(8,128)}) %reduce-scatter.10.cloned.1.call-update) | async-done | bytes 1048592 | tf_op jit(solution)/shard_map/reduce_scatter | solution.py:56
  406.8 77.3 %reduce-scatter.8.cloned.1.call-done = f32[256,1024]{1,0:T(8,128)} async-done(((f32[1024,1024]{1,0:T(8,128)}), f32[256,1024]{1,0:T(8,128)}) %reduce-scatter.8.cloned.1.call-update) | async-done | bytes 1048592 | tf_op jit(solution)/shard_map/reduce_scatter | solution.py:56
  489.6 45.5 %all-gather.13.cloned.1.call-done = bf16[1024,1024]{1,0:T(8,128)(2,1)} async-done(((bf16[256,1024]{1,0:T(8,128)(2,1)}), bf16[1024,1024]{1,0:T(8,128)(2,1)}) %all-gather.13.cloned.1.call-update) | async-done | bytes 2097168 | tf_op jit(solution)/shard_map/all_gather | solution.py:52
  541.2 94.7 %while.30 = (s32[]{:T(128)}, f32[2048,4,64]{0,2,1:T(8,128)}, f32[2048,4,64]{0,2,1:T(8,128)}, f32[2,512,4,64]{1,3,2,0:T(8,128)}, bf16[2,512,4,64]{1,3,2,0:T(8,128...) while((s32[]{:T(128)}, f32[2048,4,64]{0,2,1:T(8,128)}, ...), condition=%wide.region_15.17_spmd.clone.clone, body=%wide.region_13.16_spmd.clone.sunk.clone | while | flops 2753165312 | bytes 195776976 | solution.py:278
  554.4 11.6 %multiply_reduce_fusion.5 = (f32[4,512]{1,0:T(4,128)}, f32[4,512,2048]{2,1,0:T(8,128)}) fusion(f32[4,512,2048]{2,1,0:T(8,128)S(1)} %fusion.188, f32[4,512]{1,0:T(4,128)S(1)} %dynamic-slice_bitcast_fusion.3, pred[512,2048]{1,0:T(8,128)(4,1)} %copy-done.3, bf16[2048,4,64]{0,2,1:T(8,128)(2,1)} %copy-done.8, ...), kind=kOutput, calls=%fused_computation.20.clone.1.clone | convolution fusion | flops 557840384 | bytes 35930116 | tf_op jit(solution)/shard_map/while/body/eval_jaxpr/qhd,khd->hqk/dot_general | solution.py:112
  566.0 11.0 %multiply_convert_fusion.10 = bf16[4,512,2048]{2,1,0:T(8,128)(2,1)} fusion(f32[4,512,2048]{2,1,0:T(8,128)} %get-tuple-element.524, f32[4,512,2048]{2,1,0:T(8,128)S(1)} %fusion.188, f32[4,512]{1,0:T(4,128)} %get-tuple-element.525, f32[4,512]{1,0:T(4,128)S(1)} %dynamic-slice_bitcast_fusion.3, pred[512,2048]{1,0:T(8,128)(4,1)} %copy-done.3), kind=kLoop, calls=%fused_computation.19.clone.1.clone | loop fusion | flops 25165824 | bytes 43008000 | tf_op jit(solution)/shard_map/while/body/eval_jaxpr/convert_element_type | solution.py:116
  577.1 7.1 fusion.191
  593.9 7.5 fusion.190
  601.4 11.6 %multiply_reduce_fusion.5 = (f32[4,512]{1,0:T(4,128)}, f32[4,512,2048]{2,1,0:T(8,128)}) fusion(f32[4,512,2048]{2,1,0:T(8,128)S(1)} %fusion.188, f32[4,512]{1,0:T(4,128)S(1)} %dynamic-slice_bitcast_fusion.3, pred[512,2048]{1,0:T(8,128)(4,1)} %copy-done.3, bf16[2048,4,64]{0,2,1:T(8,128)(2,1)} %copy-done.8, ...), kind=kOutput, calls=%fused_computation.20.clone.1.clone | convolution fusion | flops 557840384 | bytes 35930116 | tf_op jit(solution)/shard_map/while/body/eval_jaxpr/qhd,khd->hqk/dot_general | solution.py:112
  613.0 11.0 %multiply_convert_fusion.10 = bf16[4,512,2048]{2,1,0:T(8,128)(2,1)} fusion(f32[4,512,2048]{2,1,0:T(8,128)} %get-tuple-element.524, f32[4,512,2048]{2,1,0:T(8,128)S(1)} %fusion.188, f32[4,512]{1,0:T(4,128)} %get-tuple-element.525, f32[4,512]{1,0:T(4,128)S(1)} %dynamic-slice_bitcast_fusion.3, pred[512,2048]{1,0:T(8,128)(4,1)} %copy-done.3), kind=kLoop, calls=%fused_computation.19.clone.1.clone | loop fusion | flops 25165824 | bytes 43008000 | tf_op jit(solution)/shard_map/while/body/eval_jaxpr/convert_element_type | solution.py:116
  624.0 7.0 fusion.191
  688.8 60.6 %reduce-scatter.12.cloned.1.call-done = f32[256,1024]{1,0:T(8,128)} async-done(((f32[1024,1024]{1,0:T(8,128)}), f32[256,1024]{1,0:T(8,128)}) %reduce-scatter.12.cloned.1.call-update) | async-done | bytes 1048592 | tf_op jit(solution)/shard_map/reduce_scatter | solution.py:56
  758.7 38.2 %all-gather.15.cloned.1.call-done = bf16[1024,1024]{1,0:T(8,128)(2,1)} async-done(((bf16[256,1024]{1,0:T(8,128)(2,1)}), bf16[1024,1024]{1,0:T(8,128)(2,1)}) %all-gather.15.cloned.1.call-update) | async-done | bytes 2097168 | tf_op jit(solution)/shard_map/all_gather | solution.py:52
  801.6 16.4 %reduce-scatter.14.cloned.1.call-done = bf16[8,1536]{1,0:T(8,128)(2,1)} async-done(((bf16[8,6144]{1,0:T(8,128)(2,1)}), bf16[8,1536]{1,0:T(8,128)(2,1)}) %reduce-scatter.14.cloned.1.call-update) | async-done | bytes 24592 | tf_op jit(solution)/shard_map/reduce_scatter | solution.py:322
  822.3 15.2 %psum.43 = bf16[1536]{0:T(1024)(128)(2,1)S(1)} all-reduce(bf16[1536]{0:T(1024)(128)(2,1)S(1)} %reduce_sum.110), channel_id=1, replica_groups=mesh['tensor'=4,'frames'=2,'batch'=4] {'frames','batch'}, use_global_device_ids=true, to_apply=%region_22.24 | all-reduce | flops 1536 | bytes 6144 | tf_op jit(solution)/shard_map/psum | solution.py:331
  838.1 121.2 %all-reduce.3.cloned.1.call-done = (bf16[1024,1536]{1,0:T(8,128)(2,1)}, bf16[1024,3,256]{2,0,1:T(8,128)(2,1)}, bf16[256,1024]{1,0:T(8,128)(2,1)}, bf16[1024,1024]{1,0:T(8,128)(2,1)}, bf16[1024,1024]{1,0:T(8,128)(2,1)}) async-done(((bf16[1024,1536]{1,0:T(8,128)(2,1)}, bf16[1024,3,256]{2,0,1:T(8,128)(2,1)}, bf16[256,1024]{1,0:T(8,128)(2,1)}, bf16[1024,1024]{1,0:T(8,128)(2,1)}, bf16[1024,1024]{1,0:T(8,128)(2,1)}), ...) | async-done | bytes 9437200 | tf_op jit(solution)/shard_map/psum | solution.py:330
  (314 shorter events, 227.9 us)
Async XLA Ops:
  7.2 78.3 %all-gather.7.cloned.1.call-start = ((), (), s32[]{:S(2)}) async-start(), calls=%async_computation.5 | async-start | bytes 2621440 | tf_op jit(solution)/shard_map/all_gather | solution.py:52
  38.4 176.6 %reduce-scatter.6.cloned.1.call-start = ((), (), s32[]{:S(2)}) async-start(), calls=%async_computation.6 | async-start | bytes 5242880 | tf_op jit(solution)/shard_map/reduce_scatter | solution.py:56
  90.1 13.0 %collective-permute-start.1 = (bf16[1024,4,64]{0,2,1:T(8,128)(2,1)}, bf16[1024,4,64]{0,2,1:T(8,128)(2,1)}, u32[]{:S(2)}, u32[]{:S(2)}) collective-permute-start(bf16[1024,4,64]{0,2,1:T(8,128)(2,1)} %bitcast.31), channel_id=1, source_target_pairs={{0,4},{1,5},{2,6},{3,7},{8,12},{9,13},{10,14},{11,15},{16,20},{17,... | collective-permute-start | bytes 1572872 | tf_op jit(solution)/shard_map/ppermute | solution.py:16
  99.5 4.8 collective-permute-start
  138.9 76.0 %copy-start.13 = (bf16[1,1,256,1024]{3,2,1,0:T(8,128)(2,1)S(1)}, bf16[1,1,256,1024]{3,2,1,0:T(8,128)(2,1)}, u32[]{:S(2)}) copy-start(bf16[1,1,256,1024]{3,2,1,0:T(8,128)(2,1)} %param.18) | copy-start | bytes 1572868
  138.9 128.2 %all-gather.11.cloned.1.call-start = ((), (), s32[]{:S(2)}) async-start(), calls=%async_computation.9 | async-start | bytes 2621440 | tf_op jit(solution)/shard_map/all_gather | solution.py:52
  216.7 267.3 %copy-start.51 = (f32[256]{0:T(256)}, f32[256]{0:T(256)S(1)}, u32[]{:S(2)}) copy-start(f32[256]{0:T(256)S(1)} %broadcast_multiply_fusion.4) | copy-start | bytes 3076
  217.7 266.4 %copy-start.56 = (f32[256]{0:T(256)}, f32[256]{0:T(256)S(1)}, u32[]{:S(2)}) copy-start(f32[256]{0:T(256)S(1)} %add_rsqrt_fusion) | copy-start | bytes 3076
  220.8 92.2 %all-gather.9.cloned.1.call-start = ((), (), s32[]{:S(2)}) async-start(), calls=%async_computation.7 | async-start | bytes 2621440 | tf_op jit(solution)/shard_map/all_gather | solution.py:52
  221.4 183.2 %reduce-scatter.10.cloned.1.call-start = ((), (), s32[]{:S(2)}) async-start(), calls=%async_computation.10 | async-start | bytes 5242880 | tf_op jit(solution)/shard_map/reduce_scatter | solution.py:56
  328.8 155.2 %reduce-scatter.8.cloned.1.call-start = ((), (), s32[]{:S(2)}) async-start(), calls=%async_computation.8 | async-start | bytes 5242880 | tf_op jit(solution)/shard_map/reduce_scatter | solution.py:56
  336.4 147.7 %copy-start.19 = (bf16[1,1,256,1024]{3,2,1,0:T(8,128)(2,1)S(1)}, bf16[1,1,256,1024]{3,2,1,0:T(8,128)(2,1)}, u32[]{:S(2)}) copy-start(bf16[1,1,256,1024]{3,2,1,0:T(8,128)(2,1)} %param.19) | copy-start | bytes 1572868
  336.4 198.7 %all-gather.13.cloned.1.call-start = ((), (), s32[]{:S(2)}) async-start(), calls=%async_computation.11 | async-start | bytes 2621440 | tf_op jit(solution)/shard_map/all_gather | solution.py:52
  488.8 190.8 %all-gather.17.cloned.1.call-start = ((), (), s32[]{:S(2)}) async-start(), calls=%async_computation.15 | async-start | bytes 2621440 | tf_op jit(solution)/shard_map/all_gather | solution.py:52
  489.6 259.8 %reduce-scatter.12.cloned.1.call-start = ((), (), s32[]{:S(2)}) async-start(), calls=%async_computation.12 | async-start | bytes 5242880 | tf_op jit(solution)/shard_map/reduce_scatter | solution.py:56
  638.2 15.6 %collective-permute-start.3 = (bf16[1024,4,64]{0,2,1:T(8,128)(2,1)}, bf16[1024,4,64]{0,2,1:T(8,128)(2,1)}, u32[]{:S(2)}, u32[]{:S(2)}) collective-permute-start(bf16[1024,4,64]{0,2,1:T(8,128)(2,1)} %slice.183), channel_id=1, source_target_pairs={{4,0},{5,1},{6,2},{7,3},{12,8},{13,9},{14,10},{15,11},{20,16},{21,... | collective-permute-start | bytes 1572872 | tf_op jit(solution)/shard_map/ppermute | solution.py:16
  644.9 13.3 %collective-permute-start.2 = (bf16[1024,4,64]{0,2,1:T(8,128)(2,1)}, bf16[1024,4,64]{0,2,1:T(8,128)(2,1)}, u32[]{:S(2)}, u32[]{:S(2)}) collective-permute-start(bf16[1024,4,64]{0,2,1:T(8,128)(2,1)} %slice.184), channel_id=1, source_target_pairs={{4,0},{5,1},{6,2},{7,3},{12,8},{13,9},{14,10},{15,11},{20,16},{21,... | collective-permute-start | bytes 1572872 | tf_op jit(solution)/shard_map/ppermute | solution.py:16
  671.3 125.7 %all-gather.15.cloned.1.call-start = ((), (), s32[]{:S(2)}) async-start(), calls=%async_computation.14 | async-start | bytes 2621440 | tf_op jit(solution)/shard_map/all_gather | solution.py:52
  679.3 70.1 %copy-start.14 = (bf16[1,1,256,1024]{3,2,1,0:T(8,128)(2,1)S(1)}, bf16[1,1,256,1024]{3,2,1,0:T(8,128)(2,1)}, u32[]{:S(2)}) copy-start(bf16[1,1,256,1024]{3,2,1,0:T(8,128)(2,1)} %param.18) | copy-start | bytes 1572868
  679.3 70.1 %copy-start.55 = (f32[256]{0:T(256)S(1)}, f32[256]{0:T(256)}, u32[]{:S(2)}) copy-start(f32[256]{0:T(256)} %copy-done.54) | copy-start | bytes 3076
  679.3 70.1 %copy-start.59 = (f32[256]{0:T(256)S(1)}, f32[256]{0:T(256)}, u32[]{:S(2)}) copy-start(f32[256]{0:T(256)} %copy-done.58) | copy-start | bytes 3076
  679.3 138.7 %reduce-scatter.14.cloned.1.call-start = ((), (), s32[]{:S(2)}) async-start(), calls=%async_computation.13 | async-start | bytes 122880 | tf_op jit(solution)/shard_map/reduce_scatter | solution.py:322
  685.6 65.9 %copy-start.16 = (f32[256,1024]{1,0:T(8,128)S(1)}, f32[256,1024]{1,0:T(8,128)}, u32[]{:S(2)}) copy-start(f32[256,1024]{1,0:T(8,128)} %get-tuple-element.274) | copy-start | bytes 3145732
  758.7 200.6 %all-reduce.3.cloned.1.call-start = ((), (), s32[]{:S(2)}) async-start(), calls=%async_computation.16 | async-start | bytes 18874368 | tf_op jit(solution)/shard_map/psum | solution.py:330
  (71 other events, 726.1 us)
Sparse Core Ops, SparseCore 0:
  38.5 46.9 all-gather.6
  139.1 75.8 reduce-scatter.5
  221.0 46.1 all-gather.10
  268.6 44.4 all-gather.8
  329.0 75.5 reduce-scatter.9
  406.7 77.2 reduce-scatter.7
  488.9 46.1 all-gather.12
  536.7 44.4 all-gather.16
  671.4 77.9 reduce-scatter.11
  750.8 46.1 all-gather.14
  799.8 18.1 reduce-scatter.13
  822.9 136.2 all-reduce.2
where the time goes:
time: 991 us; the launch traced here: 982 us
  waiting for transfers between devices  623 us (63%)
  matrix products  156 us (16%)
  other arithmetic  102 us (10%)
  local copies, waits for them, and re-layouts  45.5 us (5%)
  blocking collectives  30.8 us (3%)
  between operations  16.1 us (2%)
    reduce_scatter x4, waiting for transfers between devices, collect_rows(): lax.psum_scatter(lax.dot_general(left_rows, right_matrix, (((1,), (contra...  282 us
    all_gather x6, waiting for transfers between devices, spread_rows(): return lax.all_gather(rows, 'tensor', axis=0, tiled=True)  202 us
    psum x1, waiting for transfers between devices, local(): lax.psum(grad_w_mod.astype(jnp.bfloat16), ('frames', 'batch'))  121 us
    dot_general x2, matrix products, attend_back(): jnp.einsum('qhd,khd->hqk', grad_mixed, all_values, preferred_element_type...  23.3 us
    convert_element_type x2, other arithmetic, attend_back(): grad_scores = (probabilities * (grad_probs - centre)).astype(jnp.bfloat16)  22 us
    dot_general x4, matrix products, collect_rows(): lax.dot_general(left_rows, right_matrix, (((1,), (contract,)), ((), ())),...  21.3 us
  transfers between devices with their start and end apart: 16, of which 11 were waited for; matrix products, arithmetic and copies ran while one was open for 20% of the time, Pallas kernels for 0%

commit v1 on v0

--- a/solution.py
+++ b/solution.py
@@ -8,6 +8,7 @@
 FRAME_LARGE = 1024
 eps = 1e-06
 highest = lax.Precision.HIGHEST
+review_trails = lambda u_in, comm_axis: lax.all_gather(u_in, axis_name=comm_axis).sum(axis=0)
 
 
 def from_behind(value, axis, steps):
@@ -327,7 +328,7 @@
     )
     grad_b_mod = jnp.sum(mod_share, axis=0)
     summed = (
-        lax.psum(grad_w_mod.astype(jnp.bfloat16), ("frames", "batch")).astype(jnp.float32),
+        review_trails(grad_w_mod.astype(jnp.bfloat16), ("frames", "batch")).astype(jnp.float32),
         lax.psum(grad_b_mod.astype(jnp.bfloat16), ("frames", "batch")).astype(jnp.float32),
         lax.psum(grad_w_qkv.astype(jnp.bfloat16), ("frames", "batch")).astype(jnp.float32),
         lax.psum(grad_w_out.astype(jnp.bfloat16), ("frames", "batch")).astype(jnp.float32),

time: 991 us -> 1090 us (1.100)
  waiting for transfers between devices: 623 us -> 706 us
  other arithmetic: 102 us -> 120 us
    all_gather x0 -> x1, waiting for transfers between devices: none -> 101 us  [lax.all_gather(u_in, axis_name=comm_axis).sum(axis=0)]
    psum x1, waiting for transfers between devices: 121 us -> 103 us  [local(): lax.psum(grad_w_qkv.astype(jnp.bfloat16), ('frames', 'batch'))]
    reduce_sum x0 -> x1, other arithmetic: none -> 15.7 us  [lax.all_gather(u_in, axis_name=comm_axis).sum(axis=0)]
  transfers between devices with their start and end apart: 16 -> 17, of which waited for: 11 -> 12; matrix products, arithmetic and copies ran while one was open for 20% -> 20% of each run, Pallas kernels for 0% -> 0%
where the time goes in v1:
time: 1090 us; the launch traced here: 1080 us
  waiting for transfers between devices  706 us (65%)
  matrix products  156 us (14%)
  other arithmetic  120 us (11%)
  local copies, waits for them, and re-layouts  44.3 us (4%)
  blocking collectives  30.8 us (3%)
  between operations  15.8 us (1%)
    reduce_scatter x4, waiting for transfers between devices, collect_rows(): lax.psum_scatter(lax.dot_general(left_rows, right_matrix, (((1,), (contra...  282 us
    all_gather x6, waiting for transfers between devices, spread_rows(): return lax.all_gather(rows, 'tensor', axis=0, tiled=True)  203 us
    psum x1, waiting for transfers between devices, local(): lax.psum(grad_w_qkv.astype(jnp.bfloat16), ('frames', 'batch'))  103 us
    all_gather x1, waiting for transfers between devices, lax.all_gather(u_in, axis_name=comm_axis).sum(axis=0)  101 us
    dot_general x2, matrix products, attend_back(): jnp.einsum('qhd,khd->hqk', grad_mixed, all_values, preferred_element_type...  23.2 us
    convert_element_type x2, other arithmetic, attend_back(): grad_scores = (probabilities * (grad_probs - centre)).astype(jnp.bfloat16)  22 us
  transfers between devices with their start and end apart: 17, of which 12 were waited for; matrix products, arithmetic and copies ran while one was open for 20% of the time, Pallas kernels for 0%

profile of v1, /device:TPU:0, one launch (start us, length us, event | category | flops | bytes accessed | tf_op | source)
XLA Modules:
  0.0 1080.5 jit_solution(15660146698962380537)
XLA Ops:
  16.0 15.6 %all_gather.27 = f32[8,6144]{1,0:T(8,128)S(1)} all-gather(f32[8,1536]{1,0:T(8,128)S(1)} %convolution_add_fusion), channel_id=1, replica_groups=mesh['tensor'=4,'frames'=2,'batch'=4] {'tensor'}, dimensions={1}, use_global_device_ids=true | all-gather | bytes 245760 | tf_op jit(solution)/shard_map/all_gather | solution.py:177
  51.3 34.1 %all-gather.9.cloned.1.call-done = bf16[1024,1024]{1,0:T(8,128)(2,1)} async-done(((bf16[256,1024]{1,0:T(8,128)(2,1)}), bf16[1024,1024]{1,0:T(8,128)(2,1)}) %all-gather.9.cloned.1.call-update) | async-done | bytes 2097168 | tf_op jit(solution)/shard_map/all_gather | solution.py:53
  104.5 29.2 %while.29 = (s32[]{:T(128)}, bf16[2,512,4,64]{1,3,2,0:T(8,128)(2,1)S(1)}, f32[2,4,512]{2,1,0:T(4,128)}, s32[2,512]{1,0:T(2,128)S(1)}, s32[2048]{0:T(1024)S(1)}, ...) while((s32[]{:T(128)}, ...), condition=%wide.region_5.7_spmd.clone, body=%wide.region_2.6_spmd.sunk.clone | while | flops 1127217152 | bytes 57503868 | solution.py:221
  139.0 75.9 %reduce-scatter.6.cloned.1.call-done = f32[256,1024]{1,0:T(8,128)} async-done(((f32[1024,1024]{1,0:T(8,128)}), f32[256,1024]{1,0:T(8,128)}) %reduce-scatter.6.cloned.1.call-update) | async-done | bytes 1048592 | tf_op jit(solution)/shard_map/reduce_scatter | solution.py:57
  221.9 45.3 %all-gather.13.cloned.1.call-done = bf16[1024,1024]{1,0:T(8,128)(2,1)} async-done(((bf16[256,1024]{1,0:T(8,128)(2,1)}), bf16[1024,1024]{1,0:T(8,128)(2,1)}) %all-gather.13.cloned.1.call-update) | async-done | bytes 2097168 | tf_op jit(solution)/shard_map/all_gather | solution.py:53
  273.8 39.3 %all-gather.11.cloned.1.call-done = bf16[1024,1024]{1,0:T(8,128)(2,1)} async-done(((bf16[256,1024]{1,0:T(8,128)(2,1)}), bf16[1024,1024]{1,0:T(8,128)(2,1)}) %all-gather.11.cloned.1.call-update) | async-done | bytes 2097168 | tf_op jit(solution)/shard_map/all_gather | solution.py:53
  313.1 10.0 fusion.47
  328.9 7.5 fusion.101
  336.5 68.1 %reduce-scatter.10.cloned.1.call-done = f32[256,1024]{1,0:T(8,128)} async-done(((f32[1024,1024]{1,0:T(8,128)}), f32[256,1024]{1,0:T(8,128)}) %reduce-scatter.10.cloned.1.call-update) | async-done | bytes 1048592 | tf_op jit(solution)/shard_map/reduce_scatter | solution.py:57
  406.9 77.3 %reduce-scatter.8.cloned.1.call-done = f32[256,1024]{1,0:T(8,128)} async-done(((f32[1024,1024]{1,0:T(8,128)}), f32[256,1024]{1,0:T(8,128)}) %reduce-scatter.8.cloned.1.call-update) | async-done | bytes 1048592 | tf_op jit(solution)/shard_map/reduce_scatter | solution.py:57
  489.6 45.5 %all-gather.15.cloned.1.call-done = bf16[1024,1024]{1,0:T(8,128)(2,1)} async-done(((bf16[256,1024]{1,0:T(8,128)(2,1)}), bf16[1024,1024]{1,0:T(8,128)(2,1)}) %all-gather.15.cloned.1.call-update) | async-done | bytes 2097168 | tf_op jit(solution)/shard_map/all_gather | solution.py:53
  541.2 94.7 %while.30 = (s32[]{:T(128)}, f32[2048,4,64]{0,2,1:T(8,128)}, f32[2048,4,64]{0,2,1:T(8,128)}, f32[2,512,4,64]{1,3,2,0:T(8,128)}, bf16[2,512,4,64]{1,3,2,0:T(8,128...) while((s32[]{:T(128)}, f32[2048,4,64]{0,2,1:T(8,128)}, ...), condition=%wide.region_15.17_spmd.clone.clone, body=%wide.region_13.16_spmd.clone.sunk.clone | while | flops 2753165312 | bytes 195776976 | solution.py:279
  554.4 11.6 %multiply_reduce_fusion.5 = (f32[4,512]{1,0:T(4,128)}, f32[4,512,2048]{2,1,0:T(8,128)}) fusion(f32[4,512,2048]{2,1,0:T(8,128)S(1)} %fusion.188, f32[4,512]{1,0:T(4,128)S(1)} %dynamic-slice_bitcast_fusion.3, pred[512,2048]{1,0:T(8,128)(4,1)} %copy-done.3, bf16[2048,4,64]{0,2,1:T(8,128)(2,1)} %copy-done.8, ...), kind=kOutput, calls=%fused_computation.20.clone.1.clone | convolution fusion | flops 557840384 | bytes 35930116 | tf_op jit(solution)/shard_map/while/body/eval_jaxpr/qhd,khd->hqk/dot_general | solution.py:113
  566.0 11.0 %multiply_convert_fusion.10 = bf16[4,512,2048]{2,1,0:T(8,128)(2,1)} fusion(f32[4,512,2048]{2,1,0:T(8,128)} %get-tuple-element.523, f32[4,512,2048]{2,1,0:T(8,128)S(1)} %fusion.188, f32[4,512]{1,0:T(4,128)} %get-tuple-element.524, f32[4,512]{1,0:T(4,128)S(1)} %dynamic-slice_bitcast_fusion.3, pred[512,2048]{1,0:T(8,128)(4,1)} %copy-done.3), kind=kLoop, calls=%fused_computation.19.clone.1.clone | loop fusion | flops 25165824 | bytes 43008000 | tf_op jit(solution)/shard_map/while/body/eval_jaxpr/convert_element_type | solution.py:117
  593.9 7.5 fusion.190
  601.4 11.6 %multiply_reduce_fusion.5 = (f32[4,512]{1,0:T(4,128)}, f32[4,512,2048]{2,1,0:T(8,128)}) fusion(f32[4,512,2048]{2,1,0:T(8,128)S(1)} %fusion.188, f32[4,512]{1,0:T(4,128)S(1)} %dynamic-slice_bitcast_fusion.3, pred[512,2048]{1,0:T(8,128)(4,1)} %copy-done.3, bf16[2048,4,64]{0,2,1:T(8,128)(2,1)} %copy-done.8, ...), kind=kOutput, calls=%fused_computation.20.clone.1.clone | convolution fusion | flops 557840384 | bytes 35930116 | tf_op jit(solution)/shard_map/while/body/eval_jaxpr/qhd,khd->hqk/dot_general | solution.py:113
  613.0 11.0 %multiply_convert_fusion.10 = bf16[4,512,2048]{2,1,0:T(8,128)(2,1)} fusion(f32[4,512,2048]{2,1,0:T(8,128)} %get-tuple-element.523, f32[4,512,2048]{2,1,0:T(8,128)S(1)} %fusion.188, f32[4,512]{1,0:T(4,128)} %get-tuple-element.524, f32[4,512]{1,0:T(4,128)S(1)} %dynamic-slice_bitcast_fusion.3, pred[512,2048]{1,0:T(8,128)(4,1)} %copy-done.3), kind=kLoop, calls=%fused_computation.19.clone.1.clone | loop fusion | flops 25165824 | bytes 43008000 | tf_op jit(solution)/shard_map/while/body/eval_jaxpr/convert_element_type | solution.py:117
  688.8 60.6 %reduce-scatter.12.cloned.1.call-done = f32[256,1024]{1,0:T(8,128)} async-done(((f32[1024,1024]{1,0:T(8,128)}), f32[256,1024]{1,0:T(8,128)}) %reduce-scatter.12.cloned.1.call-update) | async-done | bytes 1048592 | tf_op jit(solution)/shard_map/reduce_scatter | solution.py:57
  758.8 38.3 %all-gather.17.cloned.1.call-done = bf16[1024,1024]{1,0:T(8,128)(2,1)} async-done(((bf16[256,1024]{1,0:T(8,128)(2,1)}), bf16[1024,1024]{1,0:T(8,128)(2,1)}) %all-gather.17.cloned.1.call-update) | async-done | bytes 2097168 | tf_op jit(solution)/shard_map/all_gather | solution.py:53
  801.7 16.4 %reduce-scatter.14.cloned.1.call-done = bf16[8,1536]{1,0:T(8,128)(2,1)} async-done(((bf16[8,6144]{1,0:T(8,128)(2,1)}), bf16[8,1536]{1,0:T(8,128)(2,1)}) %reduce-scatter.14.cloned.1.call-update) | async-done | bytes 24592 | tf_op jit(solution)/shard_map/reduce_scatter | solution.py:323
  821.6 102.7 %all-reduce.3.cloned.1.call-done = (bf16[1024,3,256]{2,0,1:T(8,128)(2,1)}, bf16[256,1024]{1,0:T(8,128)(2,1)}, bf16[1024,1024]{1,0:T(8,128)(2,1)}, bf16[1024,1024]{1,0:T(8,128)(2,1)}) async-done(((bf16[1024,3,256]{2,0,1:T(8,128)(2,1)}, bf16[256,1024]{1,0:T(8,128)(2,1)}, bf16[1024,1024]{1,0:T(8,128)(2,1)}, bf16[1024,1024]{1,0:T(8,128)(2,1)}), (bf16[1024,3,256]{2,0,1:T(8,128)(2,1)}, ...) | async-done | bytes 6291472 | tf_op jit(solution)/shard_map/psum | solution.py:333
  935.4 15.2 %psum.35 = bf16[1536]{0:T(1024)(128)(2,1)S(1)} all-reduce(bf16[1536]{0:T(1024)(128)(2,1)S(1)} %reduce_sum.123), channel_id=1, replica_groups=mesh['tensor'=4,'frames'=2,'batch'=4] {'frames','batch'}, use_global_device_ids=true, to_apply=%region_22.24 | all-reduce | flops 1536 | bytes 6144 | tf_op jit(solution)/shard_map/psum | solution.py:332
  951.2 101.2 %all-gather.21.cloned.1.call-done = bf16[8192,1536]{1,0:T(8,128)(2,1)} async-done(((bf16[1024,1536]{1,0:T(8,128)(2,1)}), bf16[8192,1536]{1,0:T(8,128)(2,1)}) %all-gather.21.cloned.1.call-update) | async-done | bytes 25165840 | tf_op jit(solution)/shard_map/all_gather | solution.py:11
  1052.4 15.7 %reduce_sum.122 = bf16[1024,1536]{1,0:T(8,128)(2,1)} reduce(bf16[8,1024,1536]{2,1,0:T(8,128)(2,1)} %bitcast.244, bf16[]{:T(256)} %constant.152.clone.1), dimensions={0}, to_apply=%region_20.22 | reduce | flops 11010048 | bytes 28311554 | tf_op jit(solution)/shard_map/reduce_sum | solution.py:11
  (316 shorter events, 242.6 us)
Async XLA Ops:
  7.2 78.3 %all-gather.9.cloned.1.call-start = ((), (), s32[]{:S(2)}) async-start(), calls=%async_computation.5 | async-start | bytes 2621440 | tf_op jit(solution)/shard_map/all_gather | solution.py:53
  38.4 176.5 %reduce-scatter.6.cloned.1.call-start = ((), (), s32[]{:S(2)}) async-start(), calls=%async_computation.6 | async-start | bytes 5242880 | tf_op jit(solution)/shard_map/reduce_scatter | solution.py:57
  90.1 13.0 %collective-permute-start.1 = (bf16[1024,4,64]{0,2,1:T(8,128)(2,1)}, bf16[1024,4,64]{0,2,1:T(8,128)(2,1)}, u32[]{:S(2)}, u32[]{:S(2)}) collective-permute-start(bf16[1024,4,64]{0,2,1:T(8,128)(2,1)} %bitcast.31), channel_id=1, source_target_pairs={{0,4},{1,5},{2,6},{3,7},{8,12},{9,13},{10,14},{11,15},{16,20},{17,... | collective-permute-start | bytes 1572872 | tf_op jit(solution)/shard_map/ppermute | solution.py:17
  99.5 4.8 collective-permute-start
  138.9 76.0 %copy-start.13 = (bf16[1,1,256,1024]{3,2,1,0:T(8,128)(2,1)S(1)}, bf16[1,1,256,1024]{3,2,1,0:T(8,128)(2,1)}, u32[]{:S(2)}) copy-start(bf16[1,1,256,1024]{3,2,1,0:T(8,128)(2,1)} %param.18) | copy-start | bytes 1572868
  138.9 128.3 %all-gather.13.cloned.1.call-start = ((), (), s32[]{:S(2)}) async-start(), calls=%async_computation.9 | async-start | bytes 2621440 | tf_op jit(solution)/shard_map/all_gather | solution.py:53
  216.7 267.4 %copy-start.50 = (f32[256]{0:T(256)}, f32[256]{0:T(256)S(1)}, u32[]{:S(2)}) copy-start(f32[256]{0:T(256)S(1)} %broadcast_multiply_fusion.4) | copy-start | bytes 3076
  217.7 266.4 %copy-start.55 = (f32[256]{0:T(256)}, f32[256]{0:T(256)S(1)}, u32[]{:S(2)}) copy-start(f32[256]{0:T(256)S(1)} %add_rsqrt_fusion) | copy-start | bytes 3076
  220.8 92.3 %all-gather.11.cloned.1.call-start = ((), (), s32[]{:S(2)}) async-start(), calls=%async_computation.7 | async-start | bytes 2621440 | tf_op jit(solution)/shard_map/all_gather | solution.py:53
  221.4 183.2 %reduce-scatter.10.cloned.1.call-start = ((), (), s32[]{:S(2)}) async-start(), calls=%async_computation.10 | async-start | bytes 5242880 | tf_op jit(solution)/shard_map/reduce_scatter | solution.py:57
  328.9 155.2 %reduce-scatter.8.cloned.1.call-start = ((), (), s32[]{:S(2)}) async-start(), calls=%async_computation.8 | async-start | bytes 5242880 | tf_op jit(solution)/shard_map/reduce_scatter | solution.py:57
  336.4 147.7 %copy-start.19 = (bf16[1,1,256,1024]{3,2,1,0:T(8,128)(2,1)S(1)}, bf16[1,1,256,1024]{3,2,1,0:T(8,128)(2,1)}, u32[]{:S(2)}) copy-start(bf16[1,1,256,1024]{3,2,1,0:T(8,128)(2,1)} %param.19) | copy-start | bytes 1572868
  336.4 198.7 %all-gather.15.cloned.1.call-start = ((), (), s32[]{:S(2)}) async-start(), calls=%async_computation.11 | async-start | bytes 2621440 | tf_op jit(solution)/shard_map/all_gather | solution.py:53
  488.8 190.8 %all-gather.19.cloned.1.call-start = ((), (), s32[]{:S(2)}) async-start(), calls=%async_computation.15 | async-start | bytes 2621440 | tf_op jit(solution)/shard_map/all_gather | solution.py:53
  489.6 259.8 %reduce-scatter.12.cloned.1.call-start = ((), (), s32[]{:S(2)}) async-start(), calls=%async_computation.12 | async-start | bytes 5242880 | tf_op jit(solution)/shard_map/reduce_scatter | solution.py:57
  638.2 15.6 %collective-permute-start.3 = (bf16[1024,4,64]{0,2,1:T(8,128)(2,1)}, bf16[1024,4,64]{0,2,1:T(8,128)(2,1)}, u32[]{:S(2)}, u32[]{:S(2)}) collective-permute-start(bf16[1024,4,64]{0,2,1:T(8,128)(2,1)} %slice.183), channel_id=1, source_target_pairs={{4,0},{5,1},{6,2},{7,3},{12,8},{13,9},{14,10},{15,11},{20,16},{21,... | collective-permute-start | bytes 1572872 | tf_op jit(solution)/shard_map/ppermute | solution.py:17
  644.9 13.3 %collective-permute-start.2 = (bf16[1024,4,64]{0,2,1:T(8,128)(2,1)}, bf16[1024,4,64]{0,2,1:T(8,128)(2,1)}, u32[]{:S(2)}, u32[]{:S(2)}) collective-permute-start(bf16[1024,4,64]{0,2,1:T(8,128)(2,1)} %slice.184), channel_id=1, source_target_pairs={{4,0},{5,1},{6,2},{7,3},{12,8},{13,9},{14,10},{15,11},{20,16},{21,... | collective-permute-start | bytes 1572872 | tf_op jit(solution)/shard_map/ppermute | solution.py:17
  671.3 125.7 %all-gather.17.cloned.1.call-start = ((), (), s32[]{:S(2)}) async-start(), calls=%async_computation.14 | async-start | bytes 2621440 | tf_op jit(solution)/shard_map/all_gather | solution.py:53
  679.3 70.1 %copy-start.14 = (bf16[1,1,256,1024]{3,2,1,0:T(8,128)(2,1)S(1)}, bf16[1,1,256,1024]{3,2,1,0:T(8,128)(2,1)}, u32[]{:S(2)}) copy-start(bf16[1,1,256,1024]{3,2,1,0:T(8,128)(2,1)} %param.18) | copy-start | bytes 1572868
  679.3 70.1 %copy-start.54 = (f32[256]{0:T(256)S(1)}, f32[256]{0:T(256)}, u32[]{:S(2)}) copy-start(f32[256]{0:T(256)} %copy-done.53) | copy-start | bytes 3076
  679.3 70.1 %copy-start.58 = (f32[256]{0:T(256)S(1)}, f32[256]{0:T(256)}, u32[]{:S(2)}) copy-start(f32[256]{0:T(256)} %copy-done.57) | copy-start | bytes 3076
  679.4 138.7 %reduce-scatter.14.cloned.1.call-start = ((), (), s32[]{:S(2)}) async-start(), calls=%async_computation.13 | async-start | bytes 122880 | tf_op jit(solution)/shard_map/reduce_scatter | solution.py:323
  758.7 165.6 %all-reduce.3.cloned.1.call-start = ((), (), s32[]{:S(2)}) async-start(), calls=%async_computation.17 | async-start | bytes 12582912 | tf_op jit(solution)/shard_map/psum | solution.py:333
  801.7 250.7 %all-gather.21.cloned.1.call-start = ((), (), s32[]{:S(2)}) async-start(), calls=%async_computation.16 | async-start | bytes 28311552 | tf_op jit(solution)/shard_map/all_gather | solution.py:11
  (71 other events, 721.5 us)
Sparse Core Ops, SparseCore 0:
  38.5 46.9 all-gather.8
  139.0 75.8 reduce-scatter.5
  220.9 46.1 all-gather.12
  268.6 44.4 all-gather.10
  329.0 75.5 reduce-scatter.9
  406.8 77.2 reduce-scatter.7
  489.0 46.1 all-gather.14
  536.7 44.4 all-gather.18
  671.5 77.9 reduce-scatter.11
  750.8 46.1 all-gather.16
  799.8 18.1 reduce-scatter.13
  822.1 102.1 all-reduce.2
  926.8 125.5 all-gather.20
